TPU v7x, 256 devices: a whole 4x4x8 slice. The times are simulated.
256 devices in a mesh: tok: 32 (over x, y, core), tp: 8 (over z).
Axes of the slice: x: 4, y: 4, z: 8, core: 2. Of those that a mesh axis runs over, the one named last changes fastest.
Arguments:
- hidden: bfloat16 [2048, 7168], P('tok'), may hold values from -6 to 6
- ln_gain: float32 [7168], replicated, may hold values from 0.1 to 1.9
- ln_bias: float32 [7168], replicated, may hold values from -3 to 3
- w_qkv: bfloat16 [7168, 3, 7168], P('tok', None, 'tp'), may hold values from -0.0625 to 0.0625
- qkv_bias: float32 [3, 7168], P(None, 'tp'), may hold values from -3 to 3
- w_out: bfloat16 [7168, 7168], P('tp', 'tok'), may hold values from -0.0625 to 0.0625
- out_bias: float32 [7168], replicated, may hold values from -3 to 3
- dec_cache: bfloat16 [64, 1024, 2, 7168], P('tok', None, None, 'tp'), may hold values from -8 to 8
- prior_kv: bfloat16 [512, 2, 2, 7168], P('tok', None, None, 'tp'), may hold values from -8 to 8
- dec_len: int32 [64], P('tok'), may hold values from 1 to 1024, as said below
- offsets: int32 [2], replicated, may hold values from 4 to 512, as said below
Outputs:
- result: bfloat16 [2048, 7168], P('tok')
- new_kv: bfloat16 [2048, 2, 7168], P('tok', None, 'tp')
Inputs may be any that keep to these rules, and one draw needn't show every extreme that they name: `dec_len`: each decode request has 1 to 1024 cached positions; some request has exactly 1024. `offsets`: each prefill block follows 4 to 512 earlier positions; one of the two follows exactly 512.
All inputs are finite; a program needn't handle non-finite values.
Results may differ from a plain program's by a relative error of at most 0.015.
Values may be sent and summed in bfloat16 or wider, within the bound.
No kernel may reach another device: no remote copies, remote signals or barrier semaphores. Data moves between devices by JAX's collectives and lax.ppermute only.
A program may use at most 128 MiB of HBM per device.

v0:
```python
import jax
import jax.numpy as jnp
from jax import lax
from jax.sharding import PartitionSpec as P

HEAD = 128
WINDOW = 512
SINKS = 4
NEG = -1e30


def attend(queries, keys, values, allowed):
    scores = jnp.einsum("qhd,khd->hqk", queries, keys, preferred_element_type=jnp.float32)
    scores = jnp.where(allowed[None], scores, NEG)
    highest = jnp.max(scores, axis=2)
    expd = jnp.where(allowed[None], jnp.exp(scores - highest[:, :, None]), 0.0)
    totals = jnp.sum(expd, axis=2)
    weighted = jnp.einsum(
        "hqk,khd->qhd", expd.astype(jnp.bfloat16), values, preferred_element_type=jnp.float32
    )
    return (highest.T, totals.T, weighted)


def combine(first, second):
    highest = jnp.maximum(first[0], second[0])
    left_scale = jnp.exp(first[0] - highest)
    right_scale = jnp.exp(second[0] - highest)
    totals = first[1] * left_scale + second[1] * right_scale
    weighted = first[2] * left_scale[:, :, None] + second[2] * right_scale[:, :, None]
    return (highest, totals, weighted)


def window_mask(query_block, query_pos, key_block, key_pos, key_valid):
    near = (key_pos[None] < SINKS) | (key_pos[None] > query_pos[:, None] - WINDOW)
    same = key_block[None] == query_block[:, None]
    return key_valid[None] & same & (key_pos[None] <= query_pos[:, None]) & near


def key_meta(devices, pre_dev, pcb, span, first_off, second_off):
    stream = devices[:, None] * pre_dev + jnp.arange(pre_dev, dtype=jnp.int32)[None]
    new_block = stream // span
    new_pos = jnp.where(new_block == 0, first_off, second_off) + stream % span
    earlier = devices[:, None, None] * pcb + jnp.arange(pcb, dtype=jnp.int32)[None, :, None]
    old_block = jnp.zeros_like(earlier) + jnp.arange(2, dtype=jnp.int32)[None, None, :]
    old_pos = earlier + jnp.zeros_like(old_block)
    old_valid = old_pos < jnp.where(old_block == 0, first_off, second_off)
    count = devices.shape[0]
    key_block = jnp.concatenate([new_block, old_block.reshape(count, 2 * pcb)], axis=1).reshape(-1)
    key_pos = jnp.concatenate([new_pos, old_pos.reshape(count, 2 * pcb)], axis=1).reshape(-1)
    key_valid = jnp.concatenate(
        [jnp.ones((count, pre_dev), bool), old_valid.reshape(count, 2 * pcb)], axis=1
    ).reshape(-1)
    return (key_block, key_pos, key_valid)


def on_device(
    hidden,
    ln_gain,
    ln_bias,
    w_qkv,
    qkv_bias,
    w_out,
    out_bias,
    dec_cache,
    prior_kv,
    dec_len,
    offsets,
):
    tok_count = lax.axis_size("tok")
    my_index = lax.axis_index("tok")
    tok_rows = hidden.shape[0]
    dec_dev = dec_cache.shape[0]
    pre_dev = tok_rows - dec_dev
    lmax = dec_cache.shape[1]
    pcb = prior_kv.shape[0]
    head_width = w_qkv.shape[2]
    heads_dev = head_width // HEAD
    span = pre_dev * tok_count // 2
    first_off = offsets[0]
    second_off = offsets[1]
    inputs = hidden.astype(jnp.float32)
    average = jnp.mean(inputs, axis=1, keepdims=True)
    spread = jnp.mean((inputs - average) ** 2, axis=1, keepdims=True)
    normed = ((inputs - average) / jnp.sqrt(spread + 1e-05) * ln_gain + ln_bias).astype(
        jnp.bfloat16
    )
    feature_cols = lax.all_to_all(normed, "tok", split_axis=1, concat_axis=0, tiled=True)
    w_matrix = w_qkv.reshape(w_qkv.shape[0], 3 * head_width)
    summed = (
        lax.psum_scatter(
            jnp.dot(feature_cols, w_matrix, preferred_element_type=jnp.float32).astype(
                jnp.bfloat16
            ),
            "tok",
            scatter_dimension=0,
            tiled=True,
        )
        .astype(jnp.float32)
        .reshape(tok_rows, 3, head_width)
        + qkv_bias[None]
    )
    factors = jnp.array([HEAD ** (-0.5), 1.0, 1.0], jnp.float32)
    qkv = (summed * factors[None, :, None]).astype(jnp.bfloat16)
    new_kv = qkv[:, 1:]
    packed = jnp.concatenate(
        [
            qkv[:pre_dev, 1:].reshape(pre_dev, 2 * head_width),
            prior_kv.reshape(pcb * 2, 2 * head_width),
        ],
        axis=0,
    )
    per_device = pre_dev + 2 * pcb
    prefill_q = qkv[:pre_dev, 0]
    stream = my_index * pre_dev + jnp.arange(pre_dev, dtype=jnp.int32)
    query_block = stream // span
    query_pos = jnp.where(query_block == 0, first_off, second_off) + stream % span
    query_heads = prefill_q.reshape(pre_dev, heads_dev, HEAD)
    initial = (
        jnp.full((pre_dev, heads_dev), NEG, jnp.float32),
        jnp.zeros((pre_dev, heads_dev), jnp.float32),
        jnp.zeros((pre_dev, heads_dev, HEAD), jnp.float32),
    )
    piece = lax.all_gather(packed, "tok", axis=0, tiled=True)
    count = piece.shape[0] // per_device
    devices = jnp.arange(count, dtype=jnp.int32)
    key_block, fold_key_pos, key_valid = key_meta(
        devices, pre_dev, pcb, span, first_off, second_off
    )
    allowed = window_mask(query_block, query_pos, key_block, fold_key_pos, key_valid)
    key_heads = piece[:, :head_width].reshape(-1, heads_dev, HEAD)
    value_heads = piece[:, head_width:].reshape(-1, heads_dev, HEAD)
    final_state = combine(initial, attend(query_heads, key_heads, value_heads, allowed))
    prefill_out = final_state[2] / final_state[1][:, :, None]
    decode_rows = []
    for request in range(dec_dev):
        query = qkv[pre_dev + request, 0].reshape(1, heads_dev, HEAD)
        own_key = qkv[pre_dev + request, 1].reshape(1, heads_dev, HEAD)
        own_value = qkv[pre_dev + request, 2].reshape(1, heads_dev, HEAD)
        length = dec_len[request]
        cache = dec_cache[request]
        state = attend(query, own_key, own_value, jnp.ones((1, 1), bool))
        key_pos = jnp.arange(lmax, dtype=jnp.int32)
        visible = (key_pos < length) & ((key_pos < SINKS) | (key_pos > length - WINDOW))
        state = combine(
            state,
            attend(
                query,
                cache[:, 0].reshape(lmax, heads_dev, HEAD),
                cache[:, 1].reshape(lmax, heads_dev, HEAD),
                visible[None],
            ),
        )
        decode_rows.append(state[2][0] / state[1][0][:, None])
    decode_out = jnp.stack(decode_rows, axis=0)
    attn = jnp.concatenate(
        [prefill_out.reshape(pre_dev, head_width), decode_out.reshape(dec_dev, head_width)], axis=0
    ).astype(jnp.bfloat16)
    partial_rows = jnp.dot(
        lax.all_gather(attn, "tok", axis=0, tiled=True), w_out, preferred_element_type=jnp.float32
    )
    partial_value = lax.all_to_all(
        partial_rows.astype(jnp.bfloat16), "tok", split_axis=0, concat_axis=1, tiled=True
    ).astype(partial_rows.dtype)
    total = lax.psum(partial_value.astype(jnp.bfloat16), "tp").astype(jnp.float32)
    result = (inputs + total + out_bias).astype(jnp.bfloat16)
    return (result, new_kv)


def solution(mesh):
    in_specs = (
        P("tok", None),
        P(),
        P(),
        P("tok", None, "tp"),
        P(None, "tp"),
        P("tp", "tok"),
        P(),
        P("tok", None, None, "tp"),
        P("tok", None, None, "tp"),
        P("tok"),
        P(),
    )
    out_specs = (P("tok", None), P("tok", None, "tp"))
    return jax.shard_map(
        on_device, mesh=mesh, in_specs=in_specs, out_specs=out_specs, check_vma=False
    )
```

profile of v0, /device:TPU:2, one launch (start us, length us, event | category | flops | bytes accessed | tf_op | source)
XLA Modules:
  0.0 426.2 jit_solution(6795876849713984688)
XLA Ops:
  7.2 1.4 convert_reduce_fusion
  8.6 1.6 fusion.10
  10.2 1.6 fusion.13
  11.9 1.5 all_to_all.28
  13.3 1.6 copy.57
  14.9 7.6 %all-to-all-start = ((bf16[64,32,224]{2,0,1:T(8,128)(2,1)}), bf16[64,32,224]{2,0,1:T(8,128)(2,1)S(1)}, u32[]{:S(2)}, u32[]{:S(2)}) async-start(bf16[64,32,224]{2,0,1:T(8,128)(2,1)} %copy.57), calls=%async_computation | async-start | bytes 2097152 | tf_op jit(solution)/shard_map/all_to_all | solution.py:87
  22.6 1.8 copy.58
  24.4 12.5 %all-to-all-done = bf16[64,32,224]{2,0,1:T(8,128)(2,1)S(1)} async-done(((bf16[64,32,224]{2,0,1:T(8,128)(2,1)}), bf16[64,32,224]{2,0,1:T(8,128)(2,1)S(1)}, u32[]{:S(2)}, u32[]{:S(2)}) %all-to-all-start) | async-done | bytes 917536 | tf_op jit(solution)/shard_map/all_to_all | solution.py:87
  36.9 5.9 %convolution_convert_fusion = bf16[2048,2688]{1,0:T(8,128)(2,1)} fusion(bf16[2048,224]{1,0:T(8,128)(2,1)S(1)} %bitcast.162, bf16[224,2688]{0,1:T(8,128)(2,1)S(1)} %bitcast.166), kind=kOutput, calls=%fused_computation | convolution fusion | flops 2471755776 | bytes 13131776 | tf_op jit(solution)/shard_map/dot_general | solution.py:91
  42.9 0.8 copy-done.4
  43.8 107.7 %reduce-scatter.2.cloned.1.call-done = bf16[64,2688]{1,0:T(8,128)(2,1)} async-done(((bf16[2048,2688]{1,0:T(8,128)(2,1)}), bf16[64,2688]{1,0:T(8,128)(2,1)}) %reduce-scatter.2.cloned.1.call-update) | async-done | bytes 344080 | tf_op jit(solution)/shard_map/reduce_scatter | solution.py:90
  151.5 1.4 reshape.577
  152.9 0.3 multiply_convert_fusion
  153.2 0.2 slice.85
  153.4 0.2 pad.10
  153.6 0.8 maximum_bitcast_fusion
  154.4 0.2 all-gather.4.cloned.1.call-start
  154.7 7.7 %fusion.91 = (bf16[1,1024,2,896]{3,2,1,0:T(2,128)(2,1)}, bf16[1,1024,2,896]{3,2,1,0:T(2,128)(2,1)}) fusion(bf16[2,1024,2,896]{3,2,1,0:T(2,128)(2,1)} %param.19), kind=kLoop, calls=%fused_computation.144 | loop fusion | bytes 14680064 | tf_op jit(solution)/shard_map/slice | solution.py:140
  162.4 9.9 %copy.90 = bf16[1,1024,2,896]{1,3,2,0:T(8,128)(2,1)} copy(bf16[1,1024,2,896]{3,2,1,0:T(2,128)(2,1)} %get-tuple-element.19) | data formatting | bytes 7340032
  172.3 9.9 %copy.89 = bf16[1,1024,2,896]{1,3,2,0:T(8,128)(2,1)} copy(bf16[1,1024,2,896]{3,2,1,0:T(2,128)(2,1)} %get-tuple-element.18) | data formatting | bytes 7340032
  182.3 0.6 fusion.95
  184.5 0.7 fusion.94
  185.1 1.3 add_select_fusion.1
  186.5 0.1 le.19
  186.6 0.1 eq.47
  186.8 1.2 compare_select_fusion.1
  188.0 0.1 select_n.101
  188.2 0.1 copy.91
  188.3 0.1 and.78
  188.5 0.6 fusion.66
  189.1 0.7 fusion.65
  189.8 1.2 broadcast_add_fusion
  191.0 4.7 %fusion.93 = (bf16[1024,1,896]{0,2,1:T(8,128)(2,1)}, bf16[1024,1,896]{0,2,1:T(8,128)(2,1)}) fusion(bf16[1024,2,896]{0,2,1:T(8,128)(2,1)} %bitcast.157), kind=kLoop, calls=%fused_computation.146 | loop fusion | bytes 7340032 | tf_op jit(solution)/shard_map/slice | solution.py:149
  195.7 1.6 fusion.92
  197.3 0.4 or_and_fusion
  197.7 0.6 slice_reduce_fusion
  198.3 0.1 reshape_squeeze.10
  198.5 0.1 fusion.60
  198.7 2.2 fusion.69
  200.9 0.1 fusion.34
  201.0 1.9 fusion.71
  202.9 0.1 fusion.33
  203.1 0.2 fusion.44
  203.3 0.2 fusion.45
  203.6 0.6 fusion.35
  204.3 0.6 fusion.37
  205.0 13.3 %all-gather.6.cloned.1.call-done = bf16[32,94,1792]{2,1,0:T(8,128)(2,1)} async-done(((bf16[1,94,1792]{2,1,0:T(8,128)(2,1)}), bf16[32,94,1792]{2,1,0:T(8,128)(2,1)}) %all-gather.6.cloned.1.call-update) | async-done | bytes 10780688 | tf_op jit(solution)/shard_map/all_gather | solution.py:123
  218.3 11.3 %reshape.581 = bf16[3008,1792]{1,0:T(8,128)(2,1)} reshape(bf16[32,94,1792]{2,1,0:T(8,128)(2,1)} %all-gather.6.cloned.1.call-done) | data formatting | bytes 21561344
  229.5 9.1 %fusion.90 = (bf16[3008,896]{1,0:T(8,128)(2,1)}, bf16[3008,896]{1,0:T(8,128)(2,1)}) fusion(bf16[3008,1792]{1,0:T(8,128)(2,1)} %reshape.581), kind=kLoop, calls=%fused_computation.143 | loop fusion | bytes 21561344 | tf_op jit(solution)/shard_map/slice | solution.py:130
  238.6 8.3 %copy.62 = bf16[3008,896]{0,1:T(8,128)(2,1)} copy(bf16[3008,896]{1,0:T(8,128)(2,1)} %get-tuple-element.17) | data formatting | bytes 10780672 | tf_op jit(solution)/shard_map/slice | solution.py:131
  246.9 8.3 %copy.59 = bf16[3008,896]{0,1:T(8,128)(2,1)} copy(bf16[3008,896]{1,0:T(8,128)(2,1)} %get-tuple-element.16) | data formatting | bytes 10780672 | tf_op jit(solution)/shard_map/slice | solution.py:130
  255.2 4.2 select_reduce_fusion
  259.4 1.5 fusion
  260.9 2.2 fusion.28
  263.3 0.7 pad_maximum_fusion
  264.1 50.0 %all-gather.4.cloned.1.call-done = bf16[2048,896]{1,0:T(8,128)(2,1)} async-done(((bf16[64,896]{1,0:T(8,128)(2,1)}), bf16[2048,896]{1,0:T(8,128)(2,1)}) %all-gather.4.cloned.1.call-update) | async-done | bytes 3670032 | tf_op jit(solution)/shard_map/all_gather | solution.py:159
  314.0 3.4 convolution_convert_fusion.1
  317.4 0.5 copy.67
  317.9 20.2 %all_to_all.38 = bf16[32,64,224]{2,1,0:T(8,128)(2,1)S(1)} all-to-all(bf16[32,64,224]{2,1,0:T(8,128)(2,1)S(1)} %bitcast.168), channel_id=1, replica_groups=mesh['tok'=32,'tp'=8] {'tok'}, dimensions={0} | all-to-all | bytes 1835008 | tf_op jit(solution)/shard_map/all_to_all | solution.py:161
  338.2 0.6 copy.68
  338.7 2.8 all_to_all.35
  341.6 0.9 slice.98
  342.5 74.7 %all-reduce.3.cloned.1.call-done = bf16[64,7168]{1,0:T(8,128)(2,1)} async-done(((bf16[64,7168]{1,0:T(8,128)(2,1)}), bf16[64,7168]{1,0:T(8,128)(2,1)}) %all-reduce.3.cloned.1.call-update) | async-done | bytes 917520 | tf_op jit(solution)/shard_map/psum | solution.py:164
  417.3 2.4 fusion.15
  (62 shorter events, 1.4 us)
Async XLA Ops:
  7.2 306.9 %copy-start = (bf16[896,224]{0,1:T(8,128)(2,1)S(1)}, bf16[896,224]{0,1:T(8,128)(2,1)}, u32[]{:S(2)}) copy-start(bf16[896,224]{0,1:T(8,128)(2,1)} %param.17) | copy-start | bytes 1204228
  14.9 22.0 %all-to-all-start = ((bf16[64,32,224]{2,0,1:T(8,128)(2,1)}), bf16[64,32,224]{2,0,1:T(8,128)(2,1)S(1)}, u32[]{:S(2)}, u32[]{:S(2)}) async-start(bf16[64,32,224]{2,0,1:T(8,128)(2,1)} %copy.57), calls=%async_computation | async-start | bytes 2097152 | tf_op jit(solution)/shard_map/all_to_all | solution.py:87
  22.5 128.9 %reduce-scatter.2.cloned.1.call-start = ((), (), s32[]{:S(2)}) async-start(), calls=%async_computation.3 | async-start | bytes 11354112 | tf_op jit(solution)/shard_map/reduce_scatter | solution.py:90
  42.8 0.9 copy-start.4
  42.8 110.0 %copy-start.6 = (f32[3,896]{1,0:T(4,128)S(1)}, f32[3,896]{1,0:T(4,128)}, u32[]{:S(2)}) copy-start(f32[3,896]{1,0:T(4,128)} %param.16) | copy-start | bytes 32260
  42.8 110.0 %copy-start.9 = (f32[3]{0:T(128)S(1)}, f32[3]{0:T(128)}, u32[]{:S(2)}) copy-start(f32[3]{0:T(128)} %constant.75.clone) | copy-start | bytes 40
  42.9 175.4 %all-gather.6.cloned.1.call-start = ((), (), s32[]{:S(2)}) async-start(), calls=%async_computation.6 | async-start | bytes 11354112 | tf_op jit(solution)/shard_map/all_gather | solution.py:123
  154.4 159.6 %all-gather.4.cloned.1.call-start = ((), (), s32[]{:S(2)}) async-start(), calls=%async_computation.4 | async-start | bytes 3784704 | tf_op jit(solution)/shard_map/all_gather | solution.py:159
  172.3 9.9 %copy-start.7 = (s32[2]{0:T(128)S(1)}, s32[2]{0:T(128)}, u32[]{:S(2)}) copy-start(s32[2]{0:T(128)} %param.21) | copy-start | bytes 28
  172.3 12.2 %copy-start.8 = (s32[2]{0:T(128)S(1)}, s32[2]{0:T(128)}, u32[]{:S(2)}) copy-start(s32[2]{0:T(128)} %param.22) | copy-start | bytes 28
  191.0 4.7 %copy-start.1 = (bf16[1,1024,2,896]{1,3,2,0:T(8,128)(2,1)S(1)}, bf16[1,1024,2,896]{1,3,2,0:T(8,128)(2,1)}, u32[]{:S(2)}) copy-start(bf16[1,1024,2,896]{1,3,2,0:T(8,128)(2,1)} %copy.89) | copy-start | bytes 11010052
  198.5 5.2 %copy-start.3 = (bf16[1024,1,896]{0,2,1:T(8,128)(2,1)S(1)}, bf16[1024,1,896]{0,2,1:T(8,128)(2,1)}, u32[]{:S(2)}) copy-start(bf16[1024,1,896]{0,2,1:T(8,128)(2,1)} %get-tuple-element.22) | copy-start | bytes 5505028
  255.2 5.8 %slice-start = ((s8[5505024]{0:T(1024)(128)(4,1)}), s8[4194304]{0:T(1024)(128)(4,1)S(1)}, s32[]{:S(2)}) async-start(s8[5505024]{0:T(1024)(128)(4,1)} %bitcast.163), calls=%async_computation.7 | async-start | bytes 8388608
  255.2 5.8 %slice-start.1 = ((s8[5505024]{0:T(1024)(128)(4,1)}), s8[1310720]{0:T(1024)(128)(4,1)S(1)}, s32[]{:S(2)}) async-start(s8[5505024]{0:T(1024)(128)(4,1)} %bitcast.163), calls=%async_computation.8 | async-start | bytes 2621440
  264.0 153.2 %all-reduce.3.cloned.1.call-start = ((), (), s32[]{:S(2)}) async-start(), calls=%async_computation.5 | async-start | bytes 1835008 | tf_op jit(solution)/shard_map/psum | solution.py:164
  317.9 99.3 %copy-start.2 = (bf16[64,7168]{1,0:T(8,128)(2,1)S(1)}, bf16[64,7168]{1,0:T(8,128)(2,1)}, u32[]{:S(2)}) copy-start(bf16[64,7168]{1,0:T(8,128)(2,1)} %param.12) | copy-start | bytes 2752516
  317.9 99.3 %copy-start.5 = (f32[7168]{0:T(1024)S(1)}, f32[7168]{0:T(1024)}, u32[]{:S(2)}) copy-start(f32[7168]{0:T(1024)} %param.18) | copy-start | bytes 86020
Sparse Core Ops, SparseCore 0:
  43.0 108.4 reduce-scatter.1
  154.6 63.6 all-gather.5
  264.1 49.8 all-gather.3
  341.7 75.4 all-reduce.2
where the time goes:
time: 428 us; the launch traced here: 426 us
  waiting for transfers between devices  258 us (60%)
  local copies, waits for them, and re-layouts  86.4 us (20%)
  matrix products  20.9 us (5%)
  blocking collectives  20.2 us (5%)
  other arithmetic  17 us (4%)
  between operations  15.4 us (4%)
  starting transfers between devices  7.97 us (2%)
    reduce_scatter x1, waiting for transfers between devices, on_device(): lax.psum_scatter(jnp.dot(feature_cols, w_matrix, preferred_element_type=j...  108 us
    psum x1, waiting for transfers between devices, on_device(): lax.psum(partial_value.astype(jnp.bfloat16), 'tp').astype(jnp.float32)  74.7 us
    all_gather x1, waiting for transfers between devices, on_device(): lax.all_gather(attn, 'tok', axis=0, tiled=True)  50 us
    unnamed x36, local copies, waits for them, and re-layouts  34.3 us
    all_to_all x1, blocking collectives, on_device(): lax.all_to_all(partial_rows.astype(jnp.bfloat16), 'tok', split_axis=0, co...  20.2 us
    slice x2, local copies, waits for them, and re-layouts, on_device(): key_heads = piece[:, :head_width].reshape(-1, heads_dev, HEAD)  17.4 us
    all_gather x1, waiting for transfers between devices, on_device(): piece = lax.all_gather(packed, 'tok', axis=0, tiled=True)  13.3 us
    all_to_all x1, waiting for transfers between devices, on_device(): lax.all_to_all(normed, 'tok', split_axis=1, concat_axis=0, tiled=True)  12.5 us
  transfers between devices with their start and end apart: 5, of which 5 were waited for; matrix products, arithmetic and copies ran while one was open for 12% of the time, Pallas kernels for 0%

commit v1 on v0

--- a/solution.py
+++ b/solution.py
@@ -84,7 +84,13 @@
     normed = ((inputs - average) / jnp.sqrt(spread + 1e-05) * ln_gain + ln_bias).astype(
         jnp.bfloat16
     )
-    feature_cols = lax.all_to_all(normed, "tok", split_axis=1, concat_axis=0, tiled=True)
+    load_points = lambda my_data, mesh_name: jnp.concatenate(
+        jax.lax.all_to_all(
+            jnp.stack(jnp.split(my_data, jax.lax.psum(1, mesh_name), axis=1)), mesh_name, 0, 0
+        ),
+        axis=0,
+    )
+    feature_cols = load_points(normed, "tok")
     w_matrix = w_qkv.reshape(w_qkv.shape[0], 3 * head_width)
     summed = (
         lax.psum_scatter(

time: 428 us -> 453 us (1.058)
  local copies, waits for them, and re-layouts: 86.4 us -> 107 us
    unnamed x36 -> x65, local copies, waits for them, and re-layouts: 34.3 us -> 57.2 us
where the time goes in v1:
time: 453 us; the launch traced here: 451 us
  waiting for transfers between devices  258 us (57%)
  local copies, waits for them, and re-layouts  107 us (24%)
  matrix products  25 us (6%)
  blocking collectives  20.2 us (4%)
  other arithmetic  17.3 us (4%)
  between operations  15.4 us (3%)
  starting transfers between devices  8.01 us (2%)
    reduce_scatter x1, waiting for transfers between devices, on_device(): lax.psum_scatter(jnp.dot(feature_cols, w_matrix, preferred_element_type=j...  108 us
    psum x1, waiting for transfers between devices, on_device(): lax.psum(partial_value.astype(jnp.bfloat16), 'tp').astype(jnp.float32)  74.7 us
    unnamed x65, local copies, waits for them, and re-layouts  57.2 us
    all_gather x1, waiting for transfers between devices, on_device(): lax.all_gather(attn, 'tok', axis=0, tiled=True)  49.7 us
    all_to_all x1, blocking collectives, on_device(): lax.all_to_all(partial_rows.astype(jnp.bfloat16), 'tok', split_axis=0, co...  20.2 us
    slice x2, local copies, waits for them, and re-layouts, on_device(): key_heads = piece[:, :head_width].reshape(-1, heads_dev, HEAD)  17.2 us
    all_gather x1, waiting for transfers between devices, on_device(): piece = lax.all_gather(packed, 'tok', axis=0, tiled=True)  13.2 us
    all_to_all x1, waiting for transfers between devices, on_device(): jax.lax.all_to_all(jnp.stack(jnp.split(my_data, jax.lax.psum(1, mesh_name...  12.5 us
  transfers between devices with their start and end apart: 5, of which 5 were waited for; matrix products, arithmetic and copies ran while one was open for 12% of the time, Pallas kernels for 0%

profile of v1, /device:TPU:2, one launch (start us, length us, event | category | flops | bytes accessed | tf_op | source)
XLA Modules:
  0.0 450.7 jit_solution(14022703478107662442)
XLA Ops:
  7.2 1.4 convert_reduce_fusion
  8.6 1.6 fusion.10
  10.2 1.6 fusion.13
  12.5 0.7 constant_dynamic-update-slice_fusion.30
  13.2 0.7 constant_dynamic-update-slice_fusion.29
  13.8 0.7 constant_dynamic-update-slice_fusion.28
  15.1 0.7 constant_dynamic-update-slice_fusion.26
  15.8 0.7 constant_dynamic-update-slice_fusion.25
  16.5 0.7 constant_dynamic-update-slice_fusion.24
  17.8 0.7 constant_dynamic-update-slice_fusion.22
  18.5 0.7 constant_dynamic-update-slice_fusion.21
  19.2 0.7 constant_dynamic-update-slice_fusion.20
  20.5 0.7 constant_dynamic-update-slice_fusion.18
  21.1 0.7 constant_dynamic-update-slice_fusion.17
  21.8 0.7 constant_dynamic-update-slice_fusion.16
  23.1 0.7 constant_dynamic-update-slice_fusion.14
  23.8 0.7 constant_dynamic-update-slice_fusion.13
  24.5 0.7 constant_dynamic-update-slice_fusion.12
  25.8 0.7 constant_dynamic-update-slice_fusion.10
  26.5 0.7 constant_dynamic-update-slice_fusion.9
  27.1 0.7 constant_dynamic-update-slice_fusion.8
  28.4 0.7 constant_dynamic-update-slice_fusion.6
  29.1 0.7 constant_dynamic-update-slice_fusion.5
  29.8 0.7 constant_dynamic-update-slice_fusion.4
  31.1 0.7 constant_dynamic-update-slice_fusion.2
  31.8 0.7 constant_dynamic-update-slice_fusion.1
  32.5 0.7 constant_dynamic-update-slice_fusion
  33.2 7.6 %all-to-all-start = ((bf16[32,64,224]{2,1,0:T(8,128)(2,1)}), bf16[32,64,224]{2,1,0:T(8,128)(2,1)S(1)}, u32[]{:S(2)}, u32[]{:S(2)}) async-start(bf16[32,64,224]{2,1,0:T(8,128)(2,1)} %constant_dynamic-update-slice_fusion), calls=%async_computation | async-start | bytes 2097152 | tf_op jit(solution)/shard_map/all_to_all | solution.py:88
  40.8 1.8 copy.54
  42.7 12.5 %all-to-all-done = bf16[32,64,224]{2,1,0:T(8,128)(2,1)S(1)} async-done(((bf16[32,64,224]{2,1,0:T(8,128)(2,1)}), bf16[32,64,224]{2,1,0:T(8,128)(2,1)S(1)}, u32[]{:S(2)}, u32[]{:S(2)}) %all-to-all-start) | async-done | bytes 917536 | tf_op jit(solution)/shard_map/all_to_all | solution.py:88
  55.2 5.9 %convolution_convert_fusion = bf16[2048,2688]{1,0:T(8,128)(2,1)} fusion(bf16[2048,224]{1,0:T(8,128)(2,1)S(1)} %bitcast.288, bf16[224,2688]{0,1:T(8,128)(2,1)S(1)} %bitcast.290), kind=kOutput, calls=%fused_computation | convolution fusion | flops 2471755776 | bytes 13131776 | tf_op jit(solution)/shard_map/dot_general | solution.py:97
  61.2 0.8 copy-done.5
  62.0 107.7 %reduce-scatter.2.cloned.1.call-done = bf16[64,2688]{1,0:T(8,128)(2,1)} async-done(((bf16[2048,2688]{1,0:T(8,128)(2,1)}), bf16[64,2688]{1,0:T(8,128)(2,1)}) %reduce-scatter.2.cloned.1.call-update) | async-done | bytes 344080 | tf_op jit(solution)/shard_map/reduce_scatter | solution.py:96
  169.7 1.4 reshape.578
  171.9 0.8 maximum_bitcast_fusion
  173.0 0.7 fusion.94
  173.7 1.4 add_select_fusion.1
  175.4 1.3 compare_select_fusion.1
  177.2 7.9 %fusion.91 = (bf16[1,1024,2,896]{3,2,1,0:T(2,128)(2,1)}, bf16[1,1024,2,896]{3,2,1,0:T(2,128)(2,1)}) fusion(bf16[2,1024,2,896]{3,2,1,0:T(2,128)(2,1)} %param.19), kind=kLoop, calls=%fused_computation.208 | loop fusion | bytes 14680064 | tf_op jit(solution)/shard_map/slice | solution.py:146
  185.2 9.9 %copy.85 = bf16[1,1024,2,896]{1,3,2,0:T(8,128)(2,1)} copy(bf16[1,1024,2,896]{3,2,1,0:T(2,128)(2,1)} %get-tuple-element.18) | data formatting | bytes 7340032
  195.0 10.0 %copy.86 = bf16[1,1024,2,896]{1,3,2,0:T(8,128)(2,1)} copy(bf16[1,1024,2,896]{3,2,1,0:T(2,128)(2,1)} %get-tuple-element.19) | data formatting | bytes 7340032
  206.9 0.7 fusion.65
  208.2 1.3 broadcast_add_fusion
  209.6 4.4 fusion.92
  214.0 1.6 fusion.93
  217.0 2.2 fusion.71
  219.3 1.9 fusion.69
  223.3 13.2 %all-gather.6.cloned.1.call-done = bf16[32,94,1792]{2,1,0:T(8,128)(2,1)} async-done(((bf16[1,94,1792]{2,1,0:T(8,128)(2,1)}), bf16[32,94,1792]{2,1,0:T(8,128)(2,1)}) %all-gather.6.cloned.1.call-update) | async-done | bytes 10780688 | tf_op jit(solution)/shard_map/all_gather | solution.py:129
  236.5 11.3 %reshape.582 = bf16[3008,1792]{1,0:T(8,128)(2,1)} reshape(bf16[32,94,1792]{2,1,0:T(8,128)(2,1)} %all-gather.6.cloned.1.call-done) | data formatting | bytes 21561344
  247.8 9.0 %fusion.90 = (bf16[3008,896]{1,0:T(8,128)(2,1)}, bf16[3008,896]{1,0:T(8,128)(2,1)}) fusion(bf16[3008,1792]{1,0:T(8,128)(2,1)} %reshape.582), kind=kLoop, calls=%fused_computation.207 | loop fusion | bytes 21561344 | tf_op jit(solution)/shard_map/slice | solution.py:136
  256.8 8.3 %copy.55 = bf16[3008,896]{0,1:T(8,128)(2,1)} copy(bf16[3008,896]{1,0:T(8,128)(2,1)} %get-tuple-element.16) | data formatting | bytes 10780672 | tf_op jit(solution)/shard_map/slice | solution.py:136
  265.0 4.1 select_reduce_fusion
  269.1 2.4 copy-done.1
  271.5 1.5 fusion
  273.0 8.3 %copy.58 = bf16[3008,896]{0,1:T(8,128)(2,1)} copy(bf16[3008,896]{1,0:T(8,128)(2,1)} %get-tuple-element.17) | data formatting | bytes 10780672 | tf_op jit(solution)/shard_map/slice | solution.py:137
  281.3 6.4 %fusion.28 = bf16[62,7,128]{2,0,1:T(8,128)(2,1)S(1)} fusion(bf16[3008,7,128]{0,2,1:T(8,128)(2,1)} %bitcast.289, f32[7,62,3008]{2,1,0:T(8,128)} %copy-done.1, f32[7,62]{1,0:T(8,128)S(1)} %get-tuple-element.39, pred[62,3008]{1,0:T(8,128)(4,1)S(1)} %or_and_fusion, f32[62,7]{0,1:T(8,128)S(1)} %get-tuple-element.29, f32[62,7]{0,1:T(8,128)S(1)} %get-tuple-element.30, ...), kind=kOutput, calls=%fused_computation.26 | convolution fusion | flops 339644928 | bytes 10916768 | tf_op jit(solution)/shard_map/hqk,khd->qhd/dot_general | solution.py:18
  287.8 0.7 pad_maximum_fusion
  288.8 49.7 %all-gather.4.cloned.1.call-done = bf16[2048,896]{1,0:T(8,128)(2,1)} async-done(((bf16[64,896]{1,0:T(8,128)(2,1)}), bf16[2048,896]{1,0:T(8,128)(2,1)}) %all-gather.4.cloned.1.call-update) | async-done | bytes 3670032 | tf_op jit(solution)/shard_map/all_gather | solution.py:165
  338.6 3.4 convolution_convert_fusion.1
  342.5 20.2 %all_to_all.24 = bf16[32,64,224]{2,1,0:T(8,128)(2,1)S(1)} all-to-all(bf16[32,64,224]{2,1,0:T(8,128)(2,1)S(1)} %bitcast.292), channel_id=1, replica_groups=mesh['tok'=32,'tp'=8] {'tok'}, dimensions={0} | all-to-all | bytes 1835008 | tf_op jit(solution)/shard_map/all_to_all | solution.py:167
  363.3 2.8 all_to_all.21
  366.1 0.9 slice.98
  367.0 74.7 %all-reduce.3.cloned.1.call-done = bf16[64,7168]{1,0:T(8,128)(2,1)} async-done(((bf16[64,7168]{1,0:T(8,128)(2,1)}), bf16[64,7168]{1,0:T(8,128)(2,1)}) %all-reduce.3.cloned.1.call-update) | async-done | bytes 917520 | tf_op jit(solution)/shard_map/psum | solution.py:170
  441.8 2.4 fusion.15
  (89 shorter events, 13.1 us)
Async XLA Ops:
  7.2 331.4 %copy-start = (bf16[896,224]{0,1:T(8,128)(2,1)S(1)}, bf16[896,224]{0,1:T(8,128)(2,1)}, u32[]{:S(2)}) copy-start(bf16[896,224]{0,1:T(8,128)(2,1)} %param.17) | copy-start | bytes 1204228
  33.2 22.0 %all-to-all-start = ((bf16[32,64,224]{2,1,0:T(8,128)(2,1)}), bf16[32,64,224]{2,1,0:T(8,128)(2,1)S(1)}, u32[]{:S(2)}, u32[]{:S(2)}) async-start(bf16[32,64,224]{2,1,0:T(8,128)(2,1)} %constant_dynamic-update-slice_fusion), calls=%async_computation | async-start | bytes 2097152 | tf_op jit(solution)/shard_map/all_to_all | solution.py:88
  40.8 128.9 %reduce-scatter.2.cloned.1.call-start = ((), (), s32[]{:S(2)}) async-start(), calls=%async_computation.3 | async-start | bytes 11354112 | tf_op jit(solution)/shard_map/reduce_scatter | solution.py:96
  61.1 0.9 copy-start.5
  61.1 110.0 %copy-start.7 = (f32[3,896]{1,0:T(4,128)S(1)}, f32[3,896]{1,0:T(4,128)}, u32[]{:S(2)}) copy-start(f32[3,896]{1,0:T(4,128)} %param.16) | copy-start | bytes 32260
  61.1 110.0 %copy-start.10 = (f32[3]{0:T(128)S(1)}, f32[3]{0:T(128)}, u32[]{:S(2)}) copy-start(f32[3]{0:T(128)} %constant.75.clone) | copy-start | bytes 40
  61.1 111.9 %copy-start.8 = (s32[2]{0:T(128)S(1)}, s32[2]{0:T(128)}, u32[]{:S(2)}) copy-start(s32[2]{0:T(128)} %param.22) | copy-start | bytes 28
  61.1 175.4 %all-gather.6.cloned.1.call-start = ((), (), s32[]{:S(2)}) async-start(), calls=%async_computation.6 | async-start | bytes 11354112 | tf_op jit(solution)/shard_map/all_gather | solution.py:129
  172.7 165.9 %all-gather.4.cloned.1.call-start = ((), (), s32[]{:S(2)}) async-start(), calls=%async_computation.4 | async-start | bytes 3784704 | tf_op jit(solution)/shard_map/all_gather | solution.py:165
  195.0 10.0 %copy-start.9 = (s32[2]{0:T(128)S(1)}, s32[2]{0:T(128)}, u32[]{:S(2)}) copy-start(s32[2]{0:T(128)} %param.21) | copy-start | bytes 28
  209.6 4.4 copy-start.2
  216.8 5.2 %copy-start.4 = (bf16[1024,1,896]{0,2,1:T(8,128)(2,1)S(1)}, bf16[1024,1,896]{0,2,1:T(8,128)(2,1)}, u32[]{:S(2)}) copy-start(bf16[1024,1,896]{0,2,1:T(8,128)(2,1)} %get-tuple-element.20) | copy-start | bytes 5505028
  269.1 2.4 copy-start.1
  288.5 153.2 %all-reduce.3.cloned.1.call-start = ((), (), s32[]{:S(2)}) async-start(), calls=%async_computation.5 | async-start | bytes 1835008 | tf_op jit(solution)/shard_map/psum | solution.py:170
  342.5 99.3 %copy-start.3 = (bf16[64,7168]{1,0:T(8,128)(2,1)S(1)}, bf16[64,7168]{1,0:T(8,128)(2,1)}, u32[]{:S(2)}) copy-start(bf16[64,7168]{1,0:T(8,128)(2,1)} %param.12) | copy-start | bytes 2752516
  342.5 99.3 %copy-start.6 = (f32[7168]{0:T(1024)S(1)}, f32[7168]{0:T(1024)}, u32[]{:S(2)}) copy-start(f32[7168]{0:T(1024)} %param.18) | copy-start | bytes 86020
Sparse Core Ops, SparseCore 0:
  61.2 108.4 reduce-scatter.1
  172.8 63.6 all-gather.5
  288.7 49.8 all-gather.3
  366.2 75.4 all-reduce.2
